TPU v7x, 32 devices: a whole 2x2x4 slice. The times are simulated.
32 devices in a mesh: row: 4 (over y, core), col: 8 (over z, x).
Axes of the slice: x: 2, y: 2, z: 4, core: 2. Of those that a mesh axis runs over, the one named last changes fastest.
Arguments:
- resid_deriv: bfloat16 [256, 512, 1024], P(('row', 'col')), may hold values from -0.03125 to 0.03125
- local_deriv: bfloat16 [256, 512, 128], P(('row', 'col'))
- inv_factor: float32 [256, 128, 128], P(('row', 'col'))
- block_ids: int32 [256, 8], P(('row', 'col')), may hold values from 0 to 31, as said below
- right_sides: float32 [4096, 256], P(('col', 'row')), may hold values from -6 to 6
- damping: float32 [4096], P(('col', 'row')), may hold values from 0.25 to 2
Outputs:
- normal: float32 [8, 4, 128, 4096], P(None, 'row', None, 'col')
- solution: float32 [4096, 256], P(('col', 'row'))
Inputs may be any that keep to these rules, and one draw needn't show every extreme that they name: `block_ids`: all 8 bundles in each aligned block of 8 rows name the same 8 distinct blocks, each bundle in its own order. Among one such set, the values block // 4 are distinct and every residue block % 4 appears exactly 2 times.
All inputs are finite; a program needn't handle non-finite values.
Results may differ from a plain program's by a relative error of at most 0.00038.
Values sent between devices are 32-bit elements; how exact they have to be, the bound alone decides.
No kernel may reach another device: no remote copies, remote signals or barrier semaphores. Data moves between devices by JAX's collectives and lax.ppermute only.
A program may use at most 128 MiB of HBM per device.

v0:
```python
import functools

import jax
import jax.numpy as jnp
from jax import lax
from jax.experimental import pallas as pl
from jax.experimental.pallas import tpu as pltpu
from jax.sharding import PartitionSpec as P


PB = 128
ITERS = 3
AHEAD = 2
PIECES = 4

cheb_low = 0.05
cheb_high = 2.0
center = (cheb_high + cheb_low) / 2.0
radius = (cheb_high - cheb_low) / 2.0
ratio = center / radius

BOTH = ("row", "col")
VMEM = pl.BlockSpec(memory_space=pltpu.VMEM)
SMEM = pl.BlockSpec(memory_space=pltpu.SMEM)
ANY = pl.BlockSpec(memory_space=pl.ANY)
HBM = pl.BlockSpec(memory_space=pltpu.HBM)
f32_dot = functools.partial(jnp.dot, preferred_element_type=jnp.float32)


def params(mib):
    return pltpu.CompilerParams(vmem_limit_bytes=mib << 20)


def split(x):
    high = x.astype(jnp.bfloat16)
    return high, (x - high.astype(jnp.float32)).astype(jnp.bfloat16)


def dot_split(a, b):
    (ah, al), (bh, bl) = a, b
    return f32_dot(ah, bh) + (f32_dot(ah, bl) + f32_dot(al, bh))


def chunk_list(capacity):
    chunks = [(0, 0, PB + 8)]
    for slot in range(1, capacity):
        chunks.append((slot, 0, PB))
    return chunks


def region_kernel(n_row, n_col, capacity, chunks, ids_in, resid, local_in, factor_in, *refs):
    outs = refs[: len(chunks)]
    bundles, _, gp = resid.shape
    blocks, n = gp // PB, factor_in.shape[2]
    refs = refs[len(chunks) :]
    cols, rows, coupled = refs[:bundles], refs[bundles : 2 * bundles], refs[2 * bundles :][:2]
    ids, raw, partial, down, across, local, factor, stage, sector, in_sem, small_sem, out_sem = refs[
        2 * bundles + 2 :
    ]

    fetch_ids = pltpu.make_async_copy(ids_in, ids, small_sem.at[0])
    fetch_local = pltpu.make_async_copy(local_in, local, small_sem.at[1])
    fetch_factor = pltpu.make_async_copy(factor_in, factor, small_sem.at[2])
    fetches = [
        pltpu.make_async_copy(resid.at[b], raw.at[b], in_sem.at[b]) for b in range(bundles)
    ]
    ahead = min(AHEAD, bundles)
    fetch_ids.start()
    for fetch in fetches[:ahead]:
        fetch.start()
    fetch_local.start()
    stage[0, :, PB:, :] = jnp.full((n_row * n_col, 8, PB), -1.0, jnp.float32)
    fetch_ids.wait()

    def arrange(b):
        fetches[b].wait()
        if b == 0:
            fetch_factor.start()
        if b + ahead < bundles:
            fetches[b + ahead].start()
        for k in range(blocks):
            rank = jnp.int32(0)
            for j in range(blocks):
                if j != k:
                    rank = rank + (ids[b, j] < ids[b, k]).astype(jnp.int32)
            if b == 0:
                sector[rank] = ids[b, k]
            block = raw[b, :, k * PB : (k + 1) * PB]
            cols[b][rank] = block
            rows[b][pl.ds(pl.multiple_of(rank * PB, PB), PB), :] = block.T

    def couple(b):
        if b == 0:
            fetch_local.wait()
        coupled[b % 2][...] = f32_dot(rows[b][...], local[b])

    def project(b):
        if b == 0:
            fetch_factor.wait()
        ch, cl = split(coupled[b % 2][...])
        fh, fl = split(factor[b])
        terms = jnp.concatenate([fh, fl], axis=1)
        parts = f32_dot(jnp.concatenate([ch, cl], axis=1), jnp.concatenate([terms, terms], axis=0))
        projected = (parts[:, :n] + parts[:, n:]).astype(jnp.bfloat16)
        across[:, b * n : (b + 1) * n] = -projected
        for p in range(blocks):
            down[p, b * n : (b + 1) * n, :] = projected[p * PB : (p + 1) * PB].T

    def gram(i, j, picked, last):
        left = [rows[b][i * PB : (i + 2) * PB, :] for b in picked]
        pair = [[cols[b][j + x] for b in picked] for x in range(2)]
        if last:
            left.append(across[i * PB : (i + 2) * PB, :])
            pair = [parts + [down[j + x]] for x, parts in enumerate(pair)]
        right = jnp.concatenate([jnp.concatenate(parts, axis=0) for parts in pair], axis=1)
        return f32_dot(jnp.concatenate(left, axis=1), right)

    pairs = [(i, j) for i in range(0, blocks, 2) for j in range(i, blocks, 2)]
    middle = bundles // 2
    steps = bundles + 2
    early = steps - middle
    for step in range(steps):
        if step >= middle:
            for at in range((step - middle) * len(pairs) // early, (step - middle + 1) * len(pairs) // early):
                partial[at] = gram(*pairs[at], range(middle), False)
        if step < bundles:
            arrange(step)
        if 1 <= step <= bundles:
            couple(step - 1)
        if step >= 2:
            project(step - 2)

    def target(g, h):
        mine, other = sector[g], sector[h]
        residue = lax.rem(mine, n_row)
        slot = jnp.int32(0)
        if g != h:
            for j in range(g):
                slot = slot + (lax.rem(sector[j], n_row) == residue).astype(jnp.int32)
        if g < h:
            slot = slot + (lax.rem(other, n_row) == residue).astype(jnp.int32)
        place = mine - residue + lax.rem(other, n_row)
        return slot, residue * n_col + lax.div(other, n_row), place

    def put(g, h, tile):
        slot, owner, place = target(g, h)
        stage[slot, owner, :PB, :] = tile
        stage[0, owner, pl.ds(PB + slot, 1), :] = jnp.full((1, PB), place.astype(jnp.float32))

    def send(g, h):
        slot, owner, _ = target(g, h)
        tile = stage.at[slot, owner, pl.ds(0, PB), :]
        for out, (at_slot, _, _) in zip(outs, chunks):

            @pl.when(slot == at_slot)
            def _():
                there = out.at[owner, pl.ds(0, PB), :]
                pltpu.make_async_copy(tile, there, out_sem.at[0]).start()

    for at, (i, j) in enumerate(pairs):
        total = partial[at] + gram(i, j, range(middle, bundles), True)
        for x in range(2):
            for y in range(2):
                tile = total[x * PB : (x + 1) * PB, y * PB : (y + 1) * PB]
                put(i + x, j + y, tile)
                if i != j:
                    put(j + y, i + x, tile.T)
        if j + 2 == blocks:
            for x in range(2):
                for h in range(blocks):
                    send(i + x, h)
    marks = pltpu.make_async_copy(
        stage.at[0, :, pl.ds(PB, 8), :], outs[0].at[:, pl.ds(PB, 8), :], out_sem.at[1]
    )
    marks.start()
    marks.wait()
    sent = stage.at[:, pl.ds(0, blocks * blocks // capacity), pl.ds(0, PB), :]
    pltpu.make_async_copy(sent, sent, out_sem.at[0]).wait()


def region(ids, resid, local, factor, n_row, n_col, capacity, chunks):
    bundles, m, gp = resid.shape
    blocks, n = ids.shape[1], local.shape[2]
    return pl.pallas_call(
        functools.partial(region_kernel, n_row, n_col, capacity, chunks),
        out_shape=[
            jax.ShapeDtypeStruct((n_row * n_col, count, PB), jnp.float32) for _, _, count in chunks
        ],
        in_specs=[HBM] * 4,
        out_specs=[HBM] * len(chunks),
        scratch_shapes=[pltpu.VMEM((blocks, m, PB), jnp.bfloat16)] * bundles
        + [pltpu.VMEM((gp, m), jnp.bfloat16)] * bundles
        + [pltpu.VMEM((gp, n), jnp.float32)] * 2
        + [
            pltpu.SMEM(ids.shape, jnp.int32),
            pltpu.VMEM(resid.shape, resid.dtype),
            pltpu.VMEM((blocks * (blocks + 2) // 8, 2 * PB, 2 * PB), jnp.float32),
            pltpu.VMEM((blocks, bundles * n, PB), jnp.bfloat16),
            pltpu.VMEM((gp, bundles * n), jnp.bfloat16),
            pltpu.VMEM(local.shape, local.dtype),
            pltpu.VMEM(factor.shape, factor.dtype),
            pltpu.VMEM((capacity, n_row * n_col, PB + 8, PB), jnp.float32),
            pltpu.SMEM((blocks,), jnp.int32),
            pltpu.SemaphoreType.DMA((bundles,)),
            pltpu.SemaphoreType.DMA((3,)),
            pltpu.SemaphoreType.DMA((2,)),
        ],
        compiler_params=params(63),
        name="region",
    )(ids, resid, local, factor)


def add_tiles(places, slot, arrived, total, first, count, start=0, size=None):
    def step(d, carry):
        place = places[d, slot]

        @pl.when(place >= 0)
        def _():
            total[place, pl.ds(first, count), :] += arrived[d, :count, :]

        return carry

    lax.fori_loop(start, start + (size or arrived.shape[0]), step, 0)


def first_kernel(where, places, arrived, damping, total, pivot, held, sem):
    fetch = pltpu.make_async_copy(arrived, held, sem)
    fetch.start()
    total[...] = jnp.zeros_like(total)
    fetch.wait()
    add_tiles(places, 0, held, total, 0, PB)
    line = lax.broadcasted_iota(jnp.int32, (PB, PB), 0)
    column = lax.broadcasted_iota(jnp.int32, (PB, PB), 1)
    corner = total[where[0]] + jnp.where(line == column, damping[...], 0.0)
    total[where[0]] = corner
    pivot[...] = corner


def first_tiles(where, places, arrived, damping, tiles):
    return pl.pallas_call(
        first_kernel,
        out_shape=[
            jax.ShapeDtypeStruct((tiles, PB, PB), jnp.float32),
            jax.ShapeDtypeStruct((PB, PB), jnp.float32),
        ],
        in_specs=[SMEM, SMEM, ANY, VMEM],
        out_specs=[VMEM, VMEM],
        scratch_shapes=[pltpu.VMEM(arrived.shape, jnp.float32), pltpu.SemaphoreType.DMA],
        compiler_params=params(24),
        name="first_tiles",
    )(where, places, arrived, damping)


def invert_kernel(factor, rhs, inverse, turned, update):
    line = lax.broadcasted_iota(jnp.int32, (PB, PB), 0)
    column = lax.broadcasted_iota(jnp.int32, (PB, PB), 1)

    def product(a, b):
        return dot_split(split(a), split(b))

    c = jnp.where(line >= column, factor[...], 0.0)
    diagonal = jnp.sum(jnp.where(line == column, c, 0.0), axis=1, keepdims=True)
    scale = 1.0 / diagonal
    unit = c * scale
    eye = jnp.where(line == column, 1.0, 0.0)
    size = 4
    near = jnp.where((line // size == column // size) & (line > column), unit, 0.0)
    second = product(near, near)
    grown = (eye - near) + product(eye - near, second)
    while size < PB:
        size *= 2
        link = jnp.where(
            (line // size == column // size) & (line // (size // 2) != column // (size // 2)), unit, 0.0
        )
        grown = grown - product(product(grown, link), grown)
    across = jnp.sum(jnp.where(line == column, c, 0.0), axis=0, keepdims=True)
    lower = grown * (1.0 / across)
    full = product(lower.T, lower)
    inverse[...] = full
    back = rhs[...].T
    turned[...] = back
    update[...] = product(back, full) / center


def invert(factor, rhs):
    wide = rhs.shape[1]
    return pl.pallas_call(
        invert_kernel,
        out_shape=[
            jax.ShapeDtypeStruct((PB, PB), jnp.float32),
            jax.ShapeDtypeStruct((wide, PB), jnp.float32),
            jax.ShapeDtypeStruct((wide, PB), jnp.float32),
        ],
        in_specs=[VMEM, VMEM],
        out_specs=[VMEM] * 3,
        compiler_params=params(8),
        name="invert",
    )(factor, rhs)


def more_kernel(slot, first, count, places, arrived, total_in, total, held, sem):
    fetch = pltpu.make_async_copy(arrived, held, sem)
    fetch.start()
    fetch.wait()
    add_tiles(places, slot, held, total, first, count)


def more_tiles(places, arrived, total, slot, first, count):
    return pl.pallas_call(
        functools.partial(more_kernel, slot, first, count),
        out_shape=jax.ShapeDtypeStruct(total.shape, jnp.float32),
        in_specs=[SMEM, ANY, VMEM],
        out_specs=VMEM,
        input_output_aliases={2: 0},
        scratch_shapes=[pltpu.VMEM(arrived.shape, jnp.float32), pltpu.SemaphoreType.DMA],
        compiler_params=params(12),
        name="more_tiles",
    )(places, arrived, total)


def half_product(where, side, vectors, high, low, both):
    half = len(vectors)
    for mask, vector in enumerate(vectors):
        at = pl.multiple_of((lax.rem(where[2], half) ^ mask) * PB, PB)
        vh, vl = split(vector[...])
        both[0, :, pl.ds(at, PB)] = vh
        both[1, :, pl.ds(at, PB)] = vl
    rows = pl.ds(pl.multiple_of((lax.div(where[2], half) ^ side) * (half * PB), half * PB), half * PB)
    return dot_split((both[0], both[1]), (high[rows, :], low[rows, :]))


def near_kernel(half, where, high, low, total, *refs):
    vectors, (near, normal, both, whole, sem) = refs[:half], refs[half:]
    n_col, n_row = whole.shape[0], whole.shape[2] // PB
    stores = []
    for a in range(n_col):
        for sub in range(n_row):
            whole[a, :, sub * PB : (sub + 1) * PB] = total[a * n_row + sub]
        stores.append(pltpu.make_async_copy(whole.at[a], normal.at[a, 0], sem.at[a]))
        stores[-1].start()
    near[...] = half_product(where, 0, vectors, high, low, both)
    for store in stores:
        store.wait()


def far_kernel(half, where, near, high, low, *refs):
    vectors, (keep, away, both) = refs[:half], refs[half:]
    result = near[...] + half_product(where, 1, vectors, high, low, both)
    odd = lax.rem(where[1], 2) == 1
    for i in range(keep.shape[0]):
        one = result[:, 2 * i * PB : (2 * i + 1) * PB]
        two = result[:, (2 * i + 1) * PB : (2 * i + 2) * PB]
        at = lax.div(where[1], 2) ^ i
        keep[at] = jnp.where(odd, two, one)
        away[at] = jnp.where(odd, one, two)


def product_scratch(vectors):
    return pltpu.VMEM((2, vectors[0].shape[0], len(vectors) * PB), jnp.bfloat16)


def near_product(where, high, low, total, vectors):
    n_col, n_row = high.shape[0] // PB, high.shape[1] // PB
    return pl.pallas_call(
        functools.partial(near_kernel, len(vectors)),
        out_shape=[
            jax.ShapeDtypeStruct((vectors[0].shape[0], high.shape[1]), jnp.float32),
            jax.ShapeDtypeStruct((n_col, 1, PB, n_row * PB), jnp.float32),
        ],
        in_specs=[SMEM, VMEM, VMEM, VMEM] + [VMEM] * len(vectors),
        out_specs=[VMEM, ANY],
        scratch_shapes=[
            product_scratch(vectors),
            pltpu.VMEM((n_col, PB, n_row * PB), jnp.float32),
            pltpu.SemaphoreType.DMA((n_col,)),
        ],
        compiler_params=params(16),
        name="near_product",
    )(where, high, low, total, *vectors)


def far_product(where, near, high, low, vectors):
    n_row = high.shape[1] // PB
    halves = jax.ShapeDtypeStruct((n_row // 2, vectors[0].shape[0], PB), jnp.float32)
    return pl.pallas_call(
        functools.partial(far_kernel, len(vectors)),
        out_shape=[halves, halves],
        in_specs=[SMEM, VMEM, VMEM, VMEM] + [VMEM] * len(vectors),
        out_specs=[VMEM] * 2,
        scratch_shapes=[product_scratch(vectors)],
        compiler_params=params(12),
        name="far_product",
    )(where, near, high, low, *vectors)


def finish_kernel(slot, first, count, half, where, places, arrived, total_in, *refs):
    vectors = refs[:half]
    high, low, near, total, held, both, in_sem, total_sem = refs[half:]
    n_col, n_row = high.shape[0] // PB, high.shape[1] // PB
    bring = pltpu.make_async_copy(total_in, total, total_sem)
    bring.start()
    pieces = PIECES if count else 0
    size = held.shape[0] // PIECES
    fetches = [
        pltpu.make_async_copy(
            arrived.at[pl.ds(p * size, size)], held.at[pl.ds(p * size, size)], in_sem.at[p]
        )
        for p in range(pieces)
    ]
    for fetch in fetches:
        fetch.start()
    bring.wait()
    for p, fetch in enumerate(fetches):
        fetch.wait()
        add_tiles(places, slot, held, total, first, count, p * size, size)
    for a in range(n_col):
        for sub in range(n_row):
            th, tl = split(total[a * n_row + sub])
            high[a * PB : (a + 1) * PB, sub * PB : (sub + 1) * PB] = th
            low[a * PB : (a + 1) * PB, sub * PB : (sub + 1) * PB] = tl
    near[...] = half_product(where, 0, vectors, high, low, both)


def finish(where, places, arrived, total, vectors, n_row, slot, first, count):
    half = len(vectors)
    n_col = 2 * half
    wide = vectors[0].shape[0]
    split_matrix = jax.ShapeDtypeStruct((n_col * PB, n_row * PB), jnp.bfloat16)
    return pl.pallas_call(
        functools.partial(finish_kernel, slot, first, count, half),
        out_shape=[
            split_matrix,
            split_matrix,
            jax.ShapeDtypeStruct((wide, n_row * PB), jnp.float32),
            jax.ShapeDtypeStruct(total.shape, jnp.float32),
        ],
        in_specs=[SMEM, SMEM, ANY, ANY] + [VMEM] * half,
        out_specs=[VMEM] * 4,
        scratch_shapes=[
            pltpu.VMEM(arrived.shape if count else (PIECES, 8, PB), jnp.float32),
            product_scratch(vectors),
            pltpu.SemaphoreType.DMA((PIECES,)),
            pltpu.SemaphoreType.DMA,
        ],
        compiler_params=params(24),
        name="finish",
    )(where, places, arrived, total, *vectors)


def swap(x, axis, mask):
    return lax.ppermute(x, axis, [(i, i ^ mask) for i in range(lax.axis_size(axis))])


def gather_columns(own):
    half = lax.axis_size("col") // 2
    far = swap(own, "col", half)
    near = [own] + [swap(own, "col", mask) for mask in range(1, half)]
    beyond = [far] + [swap(far, "col", mask) for mask in range(1, half)]
    return near, beyond


def sum_rows(keep, away):
    mask = 1
    while True:
        summed = keep + swap(away, "row", mask)
        mask *= 2
        if mask == lax.axis_size("row"):
            return summed[0]
        keep, away = summed[0::2], summed[1::2]


def exchange(x):
    return lax.all_to_all(x, BOTH, split_axis=0, concat_axis=0, tiled=True)


def body(resid_deriv, local_deriv, inv_factor, block_ids, right_sides, damping):
    n_row, n_col = lax.axis_size("row"), lax.axis_size("col")
    devices = n_row * n_col
    capacity = max(block_ids.shape[1] // n_row, 1)
    chunks = chunk_list(capacity)
    row_index, col_index = lax.axis_index("row"), lax.axis_index("col")
    where = jnp.stack([col_index * n_row + row_index, row_index, col_index]).astype(jnp.int32)

    sends = region(
        block_ids, resid_deriv, local_deriv, inv_factor, n_row, n_col, capacity, chunks
    )
    arrived = []
    for x in sends:
        arrived.append(exchange(x))
    places = arrived[0][:, PB : PB + capacity, 0].astype(jnp.int32)

    total, pivot = first_tiles(where, places, arrived[0], damping[None, :], devices)
    factor = lax.linalg.cholesky(pivot, symmetrize_input=False)
    inverse, residual, update = invert(factor, right_sides)
    close, beyond = gather_columns(update)

    for (slot, first, count), x in list(zip(chunks, arrived))[1:-1]:
        total = more_tiles(places, x, total, slot, first, count)
    slot, first, count = chunks[-1]
    high, low, near, total = finish(
        where, places, arrived[-1], total, close, n_row, slot, first, count if slot else 0
    )
    high_dot = functools.partial(jnp.dot, precision=lax.Precision.HIGHEST)
    keep, away = far_product(where, near, high, low, beyond)
    answer = update
    weight = 1.0 / ratio
    for sweep in range(1, ITERS):
        residual = residual - sum_rows(keep, away)
        weight_next = 1.0 / (2.0 * ratio - weight)
        update = weight_next * weight * update + 2.0 * weight_next / radius * high_dot(
            residual, inverse
        )
        weight = weight_next
        answer = answer + update
        if sweep + 1 < ITERS:
            close, beyond = gather_columns(update)
            near, normal = near_product(where, high, low, total, close)
            keep, away = far_product(where, near, high, low, beyond)
    return normal, answer.T


def solution(mesh):
    return jax.shard_map(
        body,
        mesh=mesh,
        in_specs=(
            P(BOTH, None, None),
            P(BOTH, None, None),
            P(BOTH, None, None),
            P(BOTH, None),
            P(("col", "row"), None),
            P(("col", "row")),
        ),
        out_specs=(P(None, "row", None, "col"), P(("col", "row"), None)),
        check_vma=False,
    )
```

profile of v0, /device:TPU:0, one launch (start us, length us, event | category | flops | bytes accessed | tf_op | source)
XLA Modules:
  0.0 179.7 jit_solution(4673945767194215588)
XLA Ops:
  0.6 16.4 %region.1 = (f32[32,136,128]{2,1,0:T(8,128)}, f32[32,128,128]{2,1,0:T(8,128)}) custom-call(s32[8,8]{1,0:T(8,128)} %ids_in.1, bf16[8,512,1024]{2,1,0:T(8,128)(2,1)} %resid.1, bf16[8,512,128]{2,1,0:T(8,128)(2,1)} %local_in.1, f32[8,128,128]{2,1,0:T(8,128)} %factor_in.1), custom_call_target="tpu_custom_call" | custom-call | tf_op jit(solution)/shard_map/region/pallas_call | solution.py:184
  17.1 60.1 %all_to_all.10.arrived = f32[32,136,128]{2,1,0:T(8,128)S(1)} all-to-all(f32[32,136,128]{2,1,0:T(8,128)} %get-tuple-element.19), channel_id=1, replica_groups=mesh['row'=4,'col'=8] {'row','col'}, dimensions={0} | all-to-all | bytes 4456448 | tf_op jit(solution)/shard_map/all_to_all | solution.py:473
  77.2 3.6 %all-to-all-start.1 = ((f32[32,128,128]{2,1,0:T(8,128)}), f32[32,128,128]{2,1,0:T(8,128)}, u32[]{:S(2)}, u32[]{:S(2)}) async-start(f32[32,128,128]{2,1,0:T(8,128)} %get-tuple-element.20), calls=%async_computation.1 | async-start | bytes 4194304 | tf_op jit(solution)/shard_map/all_to_all | solution.py:473
  81.1 1.9 %first_tiles.1 = (f32[32,128,128]{2,1,0:T(8,128)S(1)}, f32[128,128]{1,0:T(8,128)S(1)}) custom-call(s32[3]{0:T(128)S(1)} %pad_add_fusion.where, s32[32,2]{1,0:T(8,128)S(1)} %copy.14.places, f32[32,136,128]{2,1,0:T(8,128)S(1)} %all_to_all.10.arrived, f32[1,128]{1,0:T(1,128)S(1)} %bitcast.24), custom_call_target="tpu_custom_call" | custom-call | tf_op jit(solution)/shard_map/first_tiles/pallas_call | solution.py:240
  83.0 1.3 copy-done
  84.3 11.7 %cholesky.18 = f32[128,128]{1,0:T(8,128)S(1)} custom-call(f32[128,128]{1,0:T(8,128)S(1)} %get-tuple-element.22), custom_call_target="Cholesky" | custom-call | tf_op jit(solution)/shard_map/cholesky | solution.py:493
  97.4 2.5 %invert.1 = (f32[128,128]{1,0:T(8,128)S(1)}, f32[256,128]{1,0:T(8,128)S(1)}, f32[256,128]{1,0:T(8,128)S(1)}) custom-call(f32[128,128]{1,0:T(8,128)S(1)} %select_select_fusion.factor, f32[128,256]{1,0:T(8,128)S(1)} %copy-done.2), custom_call_target="tpu_custom_call" | custom-call | tf_op jit(solution)/shard_map/invert/pallas_call | solution.py:287
  99.8 2.6 %collective-permute-start.3 = (f32[256,128]{1,0:T(8,128)S(1)}, f32[256,128]{1,0:T(8,128)S(1)}, u32[]{:S(2)}, u32[]{:S(2)}) collective-permute-start(f32[256,128]{1,0:T(8,128)S(1)} %get-tuple-element.23.refs_0_), channel_id=1, source_target_pairs={{0,4},{1,5},{2,6},{3,7},{4,0},{5,1},{6,2},{7,3},{8,12},{9,13},{10,... | collective-permute-start | bytes 393224 | tf_op jit(solution)/shard_map/ppermute | solution.py:451
  102.5 1.5 collective-permute-start
  104.0 1.5 collective-permute-start.1
  106.0 28.9 %collective-permute-done.3.refs_0_ = f32[256,128]{1,0:T(8,128)S(1)} collective-permute-done((f32[256,128]{1,0:T(8,128)S(1)}, f32[256,128]{1,0:T(8,128)S(1)}, u32[]{:S(2)}, u32[]{:S(2)}) %collective-permute-start.3) | collective-permute-done | bytes 131104 | tf_op jit(solution)/shard_map/ppermute | solution.py:451
  134.9 1.5 collective-permute-start.4
  136.4 2.0 %collective-permute-start.6 = (f32[256,128]{1,0:T(8,128)S(1)}, f32[256,128]{1,0:T(8,128)S(1)}, u32[]{:S(2)}, u32[]{:S(2)}) collective-permute-start(f32[256,128]{1,0:T(8,128)S(1)} %collective-permute-done.3.refs_0_), channel_id=1, source_target_pairs={{0,3},{1,2},{2,1},{3,0},{4,7},{5,6},{6,5},{7,4},{8,11},{9,10},{10,... | collective-permute-start | bytes 393224 | tf_op jit(solution)/shard_map/ppermute | solution.py:451
  138.4 1.6 copy-done.1
  140.0 3.7 %finish.1 = (bf16[1024,512]{1,0:T(8,128)(2,1)S(1)}, bf16[1024,512]{1,0:T(8,128)(2,1)S(1)}, f32[256,512]{1,0:T(8,128)S(1)}, f32[32,128,128]{2,1,0:T(8,128)S(1)}) custom-call(s32[3]{0:T(128)S(1)} %pad_add_fusion.where, s32[32,2]{1,0:T(8,128)S(1)} %copy.14.places, f32[32,128,128]{2,1,0:T(8,128)} %all-to-all-done.1.arrived, f32[32,128,128]{2,1,0:T(8,128)S(1)} %copy-done.1, ...), custom_call_target="tpu_custom_call" | custom-call | tf_op jit(solution)/shard_map/finish/pallas_call | solution.py:429
  143.9 1.2 far_product.2
  145.2 1.5 collective-permute-done.7
  146.8 1.6 collective-permute-start.8
  148.3 4.0 %collective-permute-done.8 = f32[1,256,128]{2,1,0:T(8,128)S(1)} collective-permute-done((f32[1,256,128]{2,1,0:T(8,128)S(1)}, f32[1,256,128]{2,1,0:T(8,128)S(1)}, u32[]{:S(2)}, u32[]{:S(2)}) %collective-permute-start.8) | collective-permute-done | bytes 131104 | tf_op jit(solution)/shard_map/ppermute | solution.py:451
  153.4 1.7 collective-permute-start.10
  155.1 1.4 collective-permute-start.11
  156.9 4.1 %collective-permute-done.12.refs_0_ = f32[256,128]{1,0:T(8,128)S(1)} collective-permute-done((f32[256,128]{1,0:T(8,128)S(1)}, f32[256,128]{1,0:T(8,128)S(1)}, u32[]{:S(2)}, u32[]{:S(2)}) %collective-permute-start.12) | collective-permute-done | bytes 131104 | tf_op jit(solution)/shard_map/ppermute | solution.py:451
  161.0 1.4 collective-permute-start.13
  162.3 2.1 %collective-permute-start.15 = (f32[256,128]{1,0:T(8,128)S(1)}, f32[256,128]{1,0:T(8,128)S(1)}, u32[]{:S(2)}, u32[]{:S(2)}) collective-permute-start(f32[256,128]{1,0:T(8,128)S(1)} %collective-permute-done.12.refs_0_), channel_id=1, source_target_pairs={{0,3},{1,2},{2,1},{3,0},{4,7},{5,6},{6,5},{7,4},{8,11},{9,10},{10,... | collective-permute-start | bytes 393224 | tf_op jit(solution)/shard_map/ppermute | solution.py:451
  164.7 2.5 %near_product.1 = (f32[256,512]{1,0:T(8,128)S(1)}, f32[8,1,128,512]{3,2,1,0:T(8,128)}) custom-call(s32[3]{0:T(128)S(1)} %pad_add_fusion.where, bf16[1024,512]{1,0:T(8,128)(2,1)S(1)} %get-tuple-element.24.high, bf16[1024,512]{1,0:T(8,128)(2,1)S(1)} %get-tuple-element.25.low, f32[32,128,128]{2,1,0:T(8,128)S(1)} %get-tuple-element.26.total, ...), custom_call_target="tpu_custom_call" | custom-call | tf_op jit(solution)/shard_map/near_product/pallas_call | solution.py:364
  167.1 1.6 collective-permute-done.13.refs_1_
  168.8 1.4 collective-permute-done.15.refs_3_
  170.2 1.2 far_product.3
  171.5 1.5 collective-permute-done.16
  173.1 1.5 collective-permute-start.17
  174.6 4.1 %collective-permute-done.17 = f32[1,256,128]{2,1,0:T(8,128)S(1)} collective-permute-done((f32[1,256,128]{2,1,0:T(8,128)S(1)}, f32[1,256,128]{2,1,0:T(8,128)S(1)}, u32[]{:S(2)}, u32[]{:S(2)}) %collective-permute-start.17) | collective-permute-done | bytes 131104 | tf_op jit(solution)/shard_map/ppermute | solution.py:451
  178.9 0.8 copy.15
  (37 shorter events, 4.2 us)
Async XLA Ops:
  77.2 3.9 %copy-start.3 = (f32[128]{0:T(128)S(1)}, f32[128]{0:T(128)}, u32[]{:S(2)}) copy-start(f32[128]{0:T(128)} %param.11) | copy-start | bytes 1540
  77.2 61.3 %all-to-all-start.1 = ((f32[32,128,128]{2,1,0:T(8,128)}), f32[32,128,128]{2,1,0:T(8,128)}, u32[]{:S(2)}, u32[]{:S(2)}) async-start(f32[32,128,128]{2,1,0:T(8,128)} %get-tuple-element.20), calls=%async_computation.1 | async-start | bytes 4194304 | tf_op jit(solution)/shard_map/all_to_all | solution.py:473
  80.8 16.6 %copy-start.2 = (f32[128,256]{1,0:T(8,128)S(1)}, f32[128,256]{1,0:T(8,128)}, u32[]{:S(2)}) copy-start(f32[128,256]{1,0:T(8,128)} %rhs.1) | copy-start | bytes 393220
  83.0 1.3 copy-start
  99.8 35.1 %collective-permute-start.3 = (f32[256,128]{1,0:T(8,128)S(1)}, f32[256,128]{1,0:T(8,128)S(1)}, u32[]{:S(2)}, u32[]{:S(2)}) collective-permute-start(f32[256,128]{1,0:T(8,128)S(1)} %get-tuple-element.23.refs_0_), channel_id=1, source_target_pairs={{0,4},{1,5},{2,6},{3,7},{4,0},{5,1},{6,2},{7,3},{8,12},{9,13},{10,... | collective-permute-start | bytes 393224 | tf_op jit(solution)/shard_map/ppermute | solution.py:451
  102.5 33.9 %collective-permute-start = (f32[256,128]{1,0:T(8,128)S(1)}, f32[256,128]{1,0:T(8,128)S(1)}, u32[]{:S(2)}, u32[]{:S(2)}) collective-permute-start(f32[256,128]{1,0:T(8,128)S(1)} %get-tuple-element.23.refs_0_), channel_id=1, source_target_pairs={{0,1},{1,0},{2,3},{3,2},{4,5},{5,4},{6,7},{7,6},{8,9},{9,8},{10,11... | collective-permute-start | bytes 393224 | tf_op jit(solution)/shard_map/ppermute | solution.py:451
  104.0 34.5 %collective-permute-start.1 = (f32[256,128]{1,0:T(8,128)S(1)}, f32[256,128]{1,0:T(8,128)S(1)}, u32[]{:S(2)}, u32[]{:S(2)}) collective-permute-start(f32[256,128]{1,0:T(8,128)S(1)} %get-tuple-element.23.refs_0_), channel_id=1, source_target_pairs={{0,2},{1,3},{2,0},{3,1},{4,6},{5,7},{6,4},{7,5},{8,10},{9,11},{10,... | collective-permute-start | bytes 393224 | tf_op jit(solution)/shard_map/ppermute | solution.py:451
  105.5 32.9 %collective-permute-start.2 = (f32[256,128]{1,0:T(8,128)S(1)}, f32[256,128]{1,0:T(8,128)S(1)}, u32[]{:S(2)}, u32[]{:S(2)}) collective-permute-start(f32[256,128]{1,0:T(8,128)S(1)} %get-tuple-element.23.refs_0_), channel_id=1, source_target_pairs={{0,3},{1,2},{2,1},{3,0},{4,7},{5,6},{6,5},{7,4},{8,11},{9,10},{10,... | collective-permute-start | bytes 393224 | tf_op jit(solution)/shard_map/ppermute | solution.py:451
  134.9 8.8 %collective-permute-start.4 = (f32[256,128]{1,0:T(8,128)S(1)}, f32[256,128]{1,0:T(8,128)S(1)}, u32[]{:S(2)}, u32[]{:S(2)}) collective-permute-start(f32[256,128]{1,0:T(8,128)S(1)} %collective-permute-done.3.refs_0_), channel_id=1, source_target_pairs={{0,1},{1,0},{2,3},{3,2},{4,5},{5,4},{6,7},{7,6},{8,9},{9,8},{10,11... | collective-permute-start | bytes 393224 | tf_op jit(solution)/shard_map/ppermute | solution.py:451
  136.4 7.4 %collective-permute-start.5 = (f32[256,128]{1,0:T(8,128)S(1)}, f32[256,128]{1,0:T(8,128)S(1)}, u32[]{:S(2)}, u32[]{:S(2)}) collective-permute-start(f32[256,128]{1,0:T(8,128)S(1)} %collective-permute-done.3.refs_0_), channel_id=1, source_target_pairs={{0,2},{1,3},{2,0},{3,1},{4,6},{5,7},{6,4},{7,5},{8,10},{9,11},{10,... | collective-permute-start | bytes 393224 | tf_op jit(solution)/shard_map/ppermute | solution.py:451
  136.4 7.5 %collective-permute-start.6 = (f32[256,128]{1,0:T(8,128)S(1)}, f32[256,128]{1,0:T(8,128)S(1)}, u32[]{:S(2)}, u32[]{:S(2)}) collective-permute-start(f32[256,128]{1,0:T(8,128)S(1)} %collective-permute-done.3.refs_0_), channel_id=1, source_target_pairs={{0,3},{1,2},{2,1},{3,0},{4,7},{5,6},{6,5},{7,4},{8,11},{9,10},{10,... | collective-permute-start | bytes 393224 | tf_op jit(solution)/shard_map/ppermute | solution.py:451
  138.4 1.6 copy-start.1
  145.1 1.6 collective-permute-start.7
  146.8 5.6 %collective-permute-start.8 = (f32[1,256,128]{2,1,0:T(8,128)S(1)}, f32[1,256,128]{2,1,0:T(8,128)S(1)}, u32[]{:S(2)}, u32[]{:S(2)}) collective-permute-start(f32[1,256,128]{2,1,0:T(8,128)S(1)} %slice.30), channel_id=1, source_target_pairs={{0,16},{8,24},{16,0},{24,8},{1,17},{9,25},{17,1},{25,9},{2,18},{10... | collective-permute-start | bytes 393224 | tf_op jit(solution)/shard_map/ppermute | solution.py:451
  152.6 8.3 %collective-permute-start.12 = (f32[256,128]{1,0:T(8,128)S(1)}, f32[256,128]{1,0:T(8,128)S(1)}, u32[]{:S(2)}, u32[]{:S(2)}) collective-permute-start(f32[256,128]{1,0:T(8,128)S(1)} %fusion.refs_0_), channel_id=1, source_target_pairs={{0,4},{1,5},{2,6},{3,7},{4,0},{5,1},{6,2},{7,3},{8,12},{9,13},{10,... | collective-permute-start | bytes 393224 | tf_op jit(solution)/shard_map/ppermute | solution.py:451
  153.4 9.0 %collective-permute-start.10 = (f32[256,128]{1,0:T(8,128)S(1)}, f32[256,128]{1,0:T(8,128)S(1)}, u32[]{:S(2)}, u32[]{:S(2)}) collective-permute-start(f32[256,128]{1,0:T(8,128)S(1)} %fusion.refs_0_), channel_id=1, source_target_pairs={{0,2},{1,3},{2,0},{3,1},{4,6},{5,7},{6,4},{7,5},{8,10},{9,11},{10,... | collective-permute-start | bytes 393224 | tf_op jit(solution)/shard_map/ppermute | solution.py:451
  155.1 9.5 %collective-permute-start.11 = (f32[256,128]{1,0:T(8,128)S(1)}, f32[256,128]{1,0:T(8,128)S(1)}, u32[]{:S(2)}, u32[]{:S(2)}) collective-permute-start(f32[256,128]{1,0:T(8,128)S(1)} %fusion.refs_0_), channel_id=1, source_target_pairs={{0,3},{1,2},{2,1},{3,0},{4,7},{5,6},{6,5},{7,4},{8,11},{9,10},{10,... | collective-permute-start | bytes 393224 | tf_op jit(solution)/shard_map/ppermute | solution.py:451
  156.6 8.1 %collective-permute-start.9 = (f32[256,128]{1,0:T(8,128)S(1)}, f32[256,128]{1,0:T(8,128)S(1)}, u32[]{:S(2)}, u32[]{:S(2)}) collective-permute-start(f32[256,128]{1,0:T(8,128)S(1)} %fusion.refs_0_), channel_id=1, source_target_pairs={{0,1},{1,0},{2,3},{3,2},{4,5},{5,4},{6,7},{7,6},{8,9},{9,8},{10,11... | collective-permute-start | bytes 393224 | tf_op jit(solution)/shard_map/ppermute | solution.py:451
  161.0 7.8 %collective-permute-start.13 = (f32[256,128]{1,0:T(8,128)S(1)}, f32[256,128]{1,0:T(8,128)S(1)}, u32[]{:S(2)}, u32[]{:S(2)}) collective-permute-start(f32[256,128]{1,0:T(8,128)S(1)} %collective-permute-done.12.refs_0_), channel_id=1, source_target_pairs={{0,1},{1,0},{2,3},{3,2},{4,5},{5,4},{6,7},{7,6},{8,9},{9,8},{10,11... | collective-permute-start | bytes 393224 | tf_op jit(solution)/shard_map/ppermute | solution.py:451
  162.3 6.5 %collective-permute-start.14 = (f32[256,128]{1,0:T(8,128)S(1)}, f32[256,128]{1,0:T(8,128)S(1)}, u32[]{:S(2)}, u32[]{:S(2)}) collective-permute-start(f32[256,128]{1,0:T(8,128)S(1)} %collective-permute-done.12.refs_0_), channel_id=1, source_target_pairs={{0,2},{1,3},{2,0},{3,1},{4,6},{5,7},{6,4},{7,5},{8,10},{9,11},{10,... | collective-permute-start | bytes 393224 | tf_op jit(solution)/shard_map/ppermute | solution.py:451
  162.3 7.9 %collective-permute-start.15 = (f32[256,128]{1,0:T(8,128)S(1)}, f32[256,128]{1,0:T(8,128)S(1)}, u32[]{:S(2)}, u32[]{:S(2)}) collective-permute-start(f32[256,128]{1,0:T(8,128)S(1)} %collective-permute-done.12.refs_0_), channel_id=1, source_target_pairs={{0,3},{1,2},{2,1},{3,0},{4,7},{5,6},{6,5},{7,4},{8,11},{9,10},{10,... | collective-permute-start | bytes 393224 | tf_op jit(solution)/shard_map/ppermute | solution.py:451
  171.4 1.6 collective-permute-start.16
  173.1 5.6 %collective-permute-start.17 = (f32[1,256,128]{2,1,0:T(8,128)S(1)}, f32[1,256,128]{2,1,0:T(8,128)S(1)}, u32[]{:S(2)}, u32[]{:S(2)}) collective-permute-start(f32[1,256,128]{2,1,0:T(8,128)S(1)} %slice.32), channel_id=1, source_target_pairs={{0,16},{8,24},{16,0},{24,8},{1,17},{9,25},{17,1},{25,9},{2,18},{10... | collective-permute-start | bytes 393224 | tf_op jit(solution)/shard_map/ppermute | solution.py:451
where the time goes:
time: 180 us
  blocking collectives  60.1 us (33%)
  waiting for transfers between devices  47.6 us (26%)
  Pallas kernels  29.5 us (16%)
  starting transfers between devices  24.2 us (13%)
  other arithmetic  13.2 us (7%)
  local copies, waits for them, and re-layouts  3.85 us (2%)
    all_to_all x1, blocking collectives, exchange(): return lax.all_to_all(x, BOTH, split_axis=0, concat_axis=0, tiled=True)  60.1 us
    ppermute x18, waiting for transfers between devices, swap(): lax.ppermute(x, axis, [(i, i ^ mask) for i in range(lax.axis_size(axis))])  47.6 us
    ppermute x18, starting transfers between devices, swap(): lax.ppermute(x, axis, [(i, i ^ mask) for i in range(lax.axis_size(axis))])  20.5 us
    pallas_call x1, Pallas kernels, region(): pl.pallas_call(functools.partial(region_kernel, n_row, n_col, capacity, c...  16.4 us
    another operation x3, other arithmetic, body(): factor = lax.linalg.cholesky(pivot, symmetrize_input=False)  12.4 us
    pallas_call x1, Pallas kernels, finish(): pl.pallas_call(functools.partial(finish_kernel, slot, first, count, half)...  3.74 us
    unnamed x9, local copies, waits for them, and re-layouts  3.65 us
    all_to_all x1, starting transfers between devices, exchange(): return lax.all_to_all(x, BOTH, split_axis=0, concat_axis=0, tiled=True)  3.61 us
  transfers between devices with their start and end apart: 19, of which 10 were waited for; matrix products, arithmetic and copies ran while one was open for 7% of the time, Pallas kernels for 6%

commit v1 on v0

--- a/solution.py
+++ b/solution.py
@@ -329,6 +329,11 @@
     return dot_split((both[0], both[1]), (high[rows, :], low[rows, :]))
 
 
+def plain_kernel(half, where, high, low, *refs):
+    vectors, (near, both) = refs[:half], refs[half:]
+    near[...] = half_product(where, 0, vectors, high, low, both)
+
+
 def near_kernel(half, where, high, low, total, *refs):
     vectors, (near, normal, both, whole, sem) = refs[:half], refs[half:]
     n_col, n_row = whole.shape[0], whole.shape[2] // PB
@@ -361,6 +366,17 @@
 
 def near_product(where, high, low, total, vectors):
     n_col, n_row = high.shape[0] // PB, high.shape[1] // PB
+    if total is None:
+        near = pl.pallas_call(
+            functools.partial(plain_kernel, len(vectors)),
+            out_shape=jax.ShapeDtypeStruct((vectors[0].shape[0], high.shape[1]), jnp.float32),
+            in_specs=[SMEM, VMEM, VMEM] + [VMEM] * len(vectors),
+            out_specs=VMEM,
+            scratch_shapes=[product_scratch(vectors)],
+            compiler_params=params(12),
+            name="first_product",
+        )(where, high, low, *vectors)
+        return near, None
     return pl.pallas_call(
         functools.partial(near_kernel, len(vectors)),
         out_shape=[
@@ -393,9 +409,8 @@
     )(where, near, high, low, *vectors)
 
 
-def finish_kernel(slot, first, count, half, where, places, arrived, total_in, *refs):
-    vectors = refs[:half]
-    high, low, near, total, held, both, in_sem, total_sem = refs[half:]
+def finish_kernel(slot, first, count, places, arrived, total_in, *refs):
+    high, low, total, held, in_sem, total_sem = refs
     n_col, n_row = high.shape[0] // PB, high.shape[1] // PB
     bring = pltpu.make_async_copy(total_in, total, total_sem)
     bring.start()
@@ -418,33 +433,27 @@
             th, tl = split(total[a * n_row + sub])
             high[a * PB : (a + 1) * PB, sub * PB : (sub + 1) * PB] = th
             low[a * PB : (a + 1) * PB, sub * PB : (sub + 1) * PB] = tl
-    near[...] = half_product(where, 0, vectors, high, low, both)
-
-
-def finish(where, places, arrived, total, vectors, n_row, slot, first, count):
-    half = len(vectors)
-    n_col = 2 * half
-    wide = vectors[0].shape[0]
+
+
+def finish(places, arrived, total, n_row, n_col, slot, first, count):
     split_matrix = jax.ShapeDtypeStruct((n_col * PB, n_row * PB), jnp.bfloat16)
     return pl.pallas_call(
-        functools.partial(finish_kernel, slot, first, count, half),
+        functools.partial(finish_kernel, slot, first, count),
         out_shape=[
             split_matrix,
             split_matrix,
-            jax.ShapeDtypeStruct((wide, n_row * PB), jnp.float32),
             jax.ShapeDtypeStruct(total.shape, jnp.float32),
         ],
-        in_specs=[SMEM, SMEM, ANY, ANY] + [VMEM] * half,
-        out_specs=[VMEM] * 4,
+        in_specs=[SMEM, ANY, ANY],
+        out_specs=[VMEM] * 3,
         scratch_shapes=[
             pltpu.VMEM(arrived.shape if count else (PIECES, 8, PB), jnp.float32),
-            product_scratch(vectors),
             pltpu.SemaphoreType.DMA((PIECES,)),
             pltpu.SemaphoreType.DMA,
         ],
         compiler_params=params(24),
         name="finish",
-    )(where, places, arrived, total, *vectors)
+    )(places, arrived, total)
 
 
 def swap(x, axis, mask):
@@ -497,9 +506,10 @@
     for (slot, first, count), x in list(zip(chunks, arrived))[1:-1]:
         total = more_tiles(places, x, total, slot, first, count)
     slot, first, count = chunks[-1]
-    high, low, near, total = finish(
-        where, places, arrived[-1], total, close, n_row, slot, first, count if slot else 0
+    high, low, total = finish(
+        places, arrived[-1], total, n_row, n_col, slot, first, count if slot else 0
     )
+    near, _ = near_product(where, high, low, None, close)
     high_dot = functools.partial(jnp.dot, precision=lax.Precision.HIGHEST)
     keep, away = far_product(where, near, high, low, beyond)
     answer = update

time: 180 us -> 181 us (level)
    pallas_call x1 -> x2, Pallas kernels: 3.74 us -> 4.17 us  [the longest x1 2.98 us: finish(): pl.pallas_call(functools.partial(finish_kernel, slot, first, count), out_...]
  transfers between devices with their start and end apart: 19 -> 19, of which waited for: 10 -> 9; matrix products, arithmetic and copies ran while one was open for 7% -> 7% of each run, Pallas kernels for 6% -> 6%
where the time goes in v1:
time: 181 us; the launch traced here: 180 us
  blocking collectives  60.1 us (33%)
  waiting for transfers between devices  48 us (27%)
  Pallas kernels  29.9 us (17%)
  starting transfers between devices  23.8 us (13%)
  other arithmetic  13.2 us (7%)
  local copies, waits for them, and re-layouts  3.86 us (2%)
    all_to_all x1, blocking collectives, exchange(): return lax.all_to_all(x, BOTH, split_axis=0, concat_axis=0, tiled=True)  60.1 us
    ppermute x18, waiting for transfers between devices, swap(): lax.ppermute(x, axis, [(i, i ^ mask) for i in range(lax.axis_size(axis))])  48 us
    ppermute x18, starting transfers between devices, swap(): lax.ppermute(x, axis, [(i, i ^ mask) for i in range(lax.axis_size(axis))])  20.2 us
    pallas_call x1, Pallas kernels, region(): pl.pallas_call(functools.partial(region_kernel, n_row, n_col, capacity, c...  16.4 us
    another operation x3, other arithmetic, body(): factor = lax.linalg.cholesky(pivot, symmetrize_input=False)  12.4 us
    unnamed x9, local copies, waits for them, and re-layouts  3.65 us
  transfers between devices with their start and end apart: 19, of which 9 were waited for; matrix products, arithmetic and copies ran while one was open for 7% of the time, Pallas kernels for 6%

profile of v1, /device:TPU:0, one launch (start us, length us, event | category | flops | bytes accessed | tf_op | source)
XLA Modules:
  0.0 180.2 jit_solution(15599816850643711247)
XLA Ops:
  0.6 16.4 %region.1 = (f32[32,136,128]{2,1,0:T(8,128)}, f32[32,128,128]{2,1,0:T(8,128)}) custom-call(s32[8,8]{1,0:T(8,128)} %ids_in.1, bf16[8,512,1024]{2,1,0:T(8,128)(2,1)} %resid.1, bf16[8,512,128]{2,1,0:T(8,128)(2,1)} %local_in.1, f32[8,128,128]{2,1,0:T(8,128)} %factor_in.1), custom_call_target="tpu_custom_call" | custom-call | tf_op jit(solution)/shard_map/region/pallas_call | solution.py:184
  17.1 60.1 %all_to_all.10.arrived = f32[32,136,128]{2,1,0:T(8,128)S(1)} all-to-all(f32[32,136,128]{2,1,0:T(8,128)} %get-tuple-element.18), channel_id=1, replica_groups=mesh['row'=4,'col'=8] {'row','col'}, dimensions={0} | all-to-all | bytes 4456448 | tf_op jit(solution)/shard_map/all_to_all | solution.py:482
  77.2 3.6 %all-to-all-start.1 = ((f32[32,128,128]{2,1,0:T(8,128)}), f32[32,128,128]{2,1,0:T(8,128)}, u32[]{:S(2)}, u32[]{:S(2)}) async-start(f32[32,128,128]{2,1,0:T(8,128)} %get-tuple-element.19), calls=%async_computation.1 | async-start | bytes 4194304 | tf_op jit(solution)/shard_map/all_to_all | solution.py:482
  81.1 1.9 %first_tiles.1 = (f32[32,128,128]{2,1,0:T(8,128)S(1)}, f32[128,128]{1,0:T(8,128)S(1)}) custom-call(s32[3]{0:T(128)S(1)} %pad_add_fusion.where, s32[32,2]{1,0:T(8,128)S(1)} %copy.14.places, f32[32,136,128]{2,1,0:T(8,128)S(1)} %all_to_all.10.arrived, f32[1,128]{1,0:T(1,128)S(1)} %bitcast.24), custom_call_target="tpu_custom_call" | custom-call | tf_op jit(solution)/shard_map/first_tiles/pallas_call | solution.py:240
  83.0 1.3 copy-done
  84.3 11.7 %cholesky.18 = f32[128,128]{1,0:T(8,128)S(1)} custom-call(f32[128,128]{1,0:T(8,128)S(1)} %get-tuple-element.24), custom_call_target="Cholesky" | custom-call | tf_op jit(solution)/shard_map/cholesky | solution.py:502
  97.4 2.5 %invert.1 = (f32[128,128]{1,0:T(8,128)S(1)}, f32[256,128]{1,0:T(8,128)S(1)}, f32[256,128]{1,0:T(8,128)S(1)}) custom-call(f32[128,128]{1,0:T(8,128)S(1)} %select_select_fusion.factor, f32[128,256]{1,0:T(8,128)S(1)} %copy-done.2), custom_call_target="tpu_custom_call" | custom-call | tf_op jit(solution)/shard_map/invert/pallas_call | solution.py:287
  99.8 2.6 %collective-permute-start.3 = (f32[256,128]{1,0:T(8,128)S(1)}, f32[256,128]{1,0:T(8,128)S(1)}, u32[]{:S(2)}, u32[]{:S(2)}) collective-permute-start(f32[256,128]{1,0:T(8,128)S(1)} %get-tuple-element.25.refs_0_), channel_id=1, source_target_pairs={{0,4},{1,5},{2,6},{3,7},{4,0},{5,1},{6,2},{7,3},{8,12},{9,13},{10,... | collective-permute-start | bytes 393224 | tf_op jit(solution)/shard_map/ppermute | solution.py:460
  102.5 1.5 collective-permute-start
  104.0 1.5 collective-permute-start.1
  106.0 28.9 %collective-permute-done.3.refs_0_ = f32[256,128]{1,0:T(8,128)S(1)} collective-permute-done((f32[256,128]{1,0:T(8,128)S(1)}, f32[256,128]{1,0:T(8,128)S(1)}, u32[]{:S(2)}, u32[]{:S(2)}) %collective-permute-start.3) | collective-permute-done | bytes 131104 | tf_op jit(solution)/shard_map/ppermute | solution.py:460
  134.9 1.5 collective-permute-start.4
  136.4 2.0 %collective-permute-start.6 = (f32[256,128]{1,0:T(8,128)S(1)}, f32[256,128]{1,0:T(8,128)S(1)}, u32[]{:S(2)}, u32[]{:S(2)}) collective-permute-start(f32[256,128]{1,0:T(8,128)S(1)} %collective-permute-done.3.refs_0_), channel_id=1, source_target_pairs={{0,3},{1,2},{2,1},{3,0},{4,7},{5,6},{6,5},{7,4},{8,11},{9,10},{10,... | collective-permute-start | bytes 393224 | tf_op jit(solution)/shard_map/ppermute | solution.py:460
  138.4 1.6 copy-done.1
  140.0 3.0 %finish.1 = (bf16[1024,512]{1,0:T(8,128)(2,1)S(1)}, bf16[1024,512]{1,0:T(8,128)(2,1)S(1)}, f32[32,128,128]{2,1,0:T(8,128)S(1)}) custom-call(s32[32,2]{1,0:T(8,128)S(1)} %copy.14.places, f32[32,128,128]{2,1,0:T(8,128)} %all-to-all-done.1.arrived, f32[32,128,128]{2,1,0:T(8,128)S(1)} %copy-done.1), custom_call_target="tpu_custom_call" | custom-call | tf_op jit(solution)/shard_map/finish/pallas_call | solution.py:440
  143.0 1.2 first_product.1.near
  144.3 1.2 far_product.2
  145.6 1.5 collective-permute-done.7
  147.1 1.6 collective-permute-start.8
  148.7 4.0 %collective-permute-done.8 = f32[1,256,128]{2,1,0:T(8,128)S(1)} collective-permute-done((f32[1,256,128]{2,1,0:T(8,128)S(1)}, f32[1,256,128]{2,1,0:T(8,128)S(1)}, u32[]{:S(2)}, u32[]{:S(2)}) %collective-permute-start.8) | collective-permute-done | bytes 131104 | tf_op jit(solution)/shard_map/ppermute | solution.py:460
  153.4 1.7 collective-permute-start.9
  155.1 1.7 collective-permute-start.10
  156.8 4.2 %collective-permute-done.12.refs_0_ = f32[256,128]{1,0:T(8,128)S(1)} collective-permute-done((f32[256,128]{1,0:T(8,128)S(1)}, f32[256,128]{1,0:T(8,128)S(1)}, u32[]{:S(2)}, u32[]{:S(2)}) %collective-permute-start.12) | collective-permute-done | bytes 131104 | tf_op jit(solution)/shard_map/ppermute | solution.py:460
  161.1 1.3 collective-permute-start.13
  162.4 2.2 %collective-permute-start.15 = (f32[256,128]{1,0:T(8,128)S(1)}, f32[256,128]{1,0:T(8,128)S(1)}, u32[]{:S(2)}, u32[]{:S(2)}) collective-permute-start(f32[256,128]{1,0:T(8,128)S(1)} %collective-permute-done.12.refs_0_), channel_id=1, source_target_pairs={{0,3},{1,2},{2,1},{3,0},{4,7},{5,6},{6,5},{7,4},{8,11},{9,10},{10,... | collective-permute-start | bytes 393224 | tf_op jit(solution)/shard_map/ppermute | solution.py:460
  164.6 1.0 collective-permute-done.11.refs_3_
  165.6 2.5 %near_product.1 = (f32[256,512]{1,0:T(8,128)S(1)}, f32[8,1,128,512]{3,2,1,0:T(8,128)}) custom-call(s32[3]{0:T(128)S(1)} %pad_add_fusion.where, bf16[1024,512]{1,0:T(8,128)(2,1)S(1)} %get-tuple-element.21.high, bf16[1024,512]{1,0:T(8,128)(2,1)S(1)} %get-tuple-element.22.low, f32[32,128,128]{2,1,0:T(8,128)S(1)} %get-tuple-element.23.total, ...), custom_call_target="tpu_custom_call" | custom-call | tf_op jit(solution)/shard_map/near_product/pallas_call | solution.py:380
  168.8 1.9 %collective-permute-done.15.refs_3_ = f32[256,128]{1,0:T(8,128)S(1)} collective-permute-done((f32[256,128]{1,0:T(8,128)S(1)}, f32[256,128]{1,0:T(8,128)S(1)}, u32[]{:S(2)}, u32[]{:S(2)}) %collective-permute-start.15) | collective-permute-done | bytes 131104 | tf_op jit(solution)/shard_map/ppermute | solution.py:460
  170.7 1.2 far_product.3
  172.0 1.5 collective-permute-done.16
  173.6 1.6 collective-permute-start.17
  175.2 4.0 %collective-permute-done.17 = f32[1,256,128]{2,1,0:T(8,128)S(1)} collective-permute-done((f32[1,256,128]{2,1,0:T(8,128)S(1)}, f32[1,256,128]{2,1,0:T(8,128)S(1)}, u32[]{:S(2)}, u32[]{:S(2)}) %collective-permute-start.17) | collective-permute-done | bytes 131104 | tf_op jit(solution)/shard_map/ppermute | solution.py:460
  (38 shorter events, 4.7 us)
Async XLA Ops:
  77.2 3.9 %copy-start.3 = (f32[128]{0:T(128)S(1)}, f32[128]{0:T(128)}, u32[]{:S(2)}) copy-start(f32[128]{0:T(128)} %param.11) | copy-start | bytes 1540
  77.2 61.3 %all-to-all-start.1 = ((f32[32,128,128]{2,1,0:T(8,128)}), f32[32,128,128]{2,1,0:T(8,128)}, u32[]{:S(2)}, u32[]{:S(2)}) async-start(f32[32,128,128]{2,1,0:T(8,128)} %get-tuple-element.19), calls=%async_computation.1 | async-start | bytes 4194304 | tf_op jit(solution)/shard_map/all_to_all | solution.py:482
  80.8 16.6 %copy-start.2 = (f32[128,256]{1,0:T(8,128)S(1)}, f32[128,256]{1,0:T(8,128)}, u32[]{:S(2)}) copy-start(f32[128,256]{1,0:T(8,128)} %rhs.1) | copy-start | bytes 393220
  83.0 1.3 copy-start
  99.8 35.1 %collective-permute-start.3 = (f32[256,128]{1,0:T(8,128)S(1)}, f32[256,128]{1,0:T(8,128)S(1)}, u32[]{:S(2)}, u32[]{:S(2)}) collective-permute-start(f32[256,128]{1,0:T(8,128)S(1)} %get-tuple-element.25.refs_0_), channel_id=1, source_target_pairs={{0,4},{1,5},{2,6},{3,7},{4,0},{5,1},{6,2},{7,3},{8,12},{9,13},{10,... | collective-permute-start | bytes 393224 | tf_op jit(solution)/shard_map/ppermute | solution.py:460
  102.5 33.9 %collective-permute-start = (f32[256,128]{1,0:T(8,128)S(1)}, f32[256,128]{1,0:T(8,128)S(1)}, u32[]{:S(2)}, u32[]{:S(2)}) collective-permute-start(f32[256,128]{1,0:T(8,128)S(1)} %get-tuple-element.25.refs_0_), channel_id=1, source_target_pairs={{0,1},{1,0},{2,3},{3,2},{4,5},{5,4},{6,7},{7,6},{8,9},{9,8},{10,11... | collective-permute-start | bytes 393224 | tf_op jit(solution)/shard_map/ppermute | solution.py:460
  104.0 39.0 %collective-permute-start.1 = (f32[256,128]{1,0:T(8,128)S(1)}, f32[256,128]{1,0:T(8,128)S(1)}, u32[]{:S(2)}, u32[]{:S(2)}) collective-permute-start(f32[256,128]{1,0:T(8,128)S(1)} %get-tuple-element.25.refs_0_), channel_id=1, source_target_pairs={{0,2},{1,3},{2,0},{3,1},{4,6},{5,7},{6,4},{7,5},{8,10},{9,11},{10,... | collective-permute-start | bytes 393224 | tf_op jit(solution)/shard_map/ppermute | solution.py:460
  105.5 37.5 %collective-permute-start.2 = (f32[256,128]{1,0:T(8,128)S(1)}, f32[256,128]{1,0:T(8,128)S(1)}, u32[]{:S(2)}, u32[]{:S(2)}) collective-permute-start(f32[256,128]{1,0:T(8,128)S(1)} %get-tuple-element.25.refs_0_), channel_id=1, source_target_pairs={{0,3},{1,2},{2,1},{3,0},{4,7},{5,6},{6,5},{7,4},{8,11},{9,10},{10,... | collective-permute-start | bytes 393224 | tf_op jit(solution)/shard_map/ppermute | solution.py:460
  134.9 9.3 %collective-permute-start.4 = (f32[256,128]{1,0:T(8,128)S(1)}, f32[256,128]{1,0:T(8,128)S(1)}, u32[]{:S(2)}, u32[]{:S(2)}) collective-permute-start(f32[256,128]{1,0:T(8,128)S(1)} %collective-permute-done.3.refs_0_), channel_id=1, source_target_pairs={{0,1},{1,0},{2,3},{3,2},{4,5},{5,4},{6,7},{7,6},{8,9},{9,8},{10,11... | collective-permute-start | bytes 393224 | tf_op jit(solution)/shard_map/ppermute | solution.py:460
  136.4 7.8 %collective-permute-start.5 = (f32[256,128]{1,0:T(8,128)S(1)}, f32[256,128]{1,0:T(8,128)S(1)}, u32[]{:S(2)}, u32[]{:S(2)}) collective-permute-start(f32[256,128]{1,0:T(8,128)S(1)} %collective-permute-done.3.refs_0_), channel_id=1, source_target_pairs={{0,2},{1,3},{2,0},{3,1},{4,6},{5,7},{6,4},{7,5},{8,10},{9,11},{10,... | collective-permute-start | bytes 393224 | tf_op jit(solution)/shard_map/ppermute | solution.py:460
  136.4 7.8 %collective-permute-start.6 = (f32[256,128]{1,0:T(8,128)S(1)}, f32[256,128]{1,0:T(8,128)S(1)}, u32[]{:S(2)}, u32[]{:S(2)}) collective-permute-start(f32[256,128]{1,0:T(8,128)S(1)} %collective-permute-done.3.refs_0_), channel_id=1, source_target_pairs={{0,3},{1,2},{2,1},{3,0},{4,7},{5,6},{6,5},{7,4},{8,11},{9,10},{10,... | collective-permute-start | bytes 393224 | tf_op jit(solution)/shard_map/ppermute | solution.py:460
  138.4 1.6 copy-start.1
  145.5 1.6 collective-permute-start.7
  147.1 5.6 %collective-permute-start.8 = (f32[1,256,128]{2,1,0:T(8,128)S(1)}, f32[1,256,128]{2,1,0:T(8,128)S(1)}, u32[]{:S(2)}, u32[]{:S(2)}) collective-permute-start(f32[1,256,128]{2,1,0:T(8,128)S(1)} %slice.30), channel_id=1, source_target_pairs={{0,16},{8,24},{16,0},{24,8},{1,17},{9,25},{17,1},{25,9},{2,18},{10... | collective-permute-start | bytes 393224 | tf_op jit(solution)/shard_map/ppermute | solution.py:460
  153.0 8.0 %collective-permute-start.12 = (f32[256,128]{1,0:T(8,128)S(1)}, f32[256,128]{1,0:T(8,128)S(1)}, u32[]{:S(2)}, u32[]{:S(2)}) collective-permute-start(f32[256,128]{1,0:T(8,128)S(1)} %fusion.refs_0_), channel_id=1, source_target_pairs={{0,4},{1,5},{2,6},{3,7},{4,0},{5,1},{6,2},{7,3},{8,12},{9,13},{10,... | collective-permute-start | bytes 393224 | tf_op jit(solution)/shard_map/ppermute | solution.py:460
  153.4 9.0 %collective-permute-start.9 = (f32[256,128]{1,0:T(8,128)S(1)}, f32[256,128]{1,0:T(8,128)S(1)}, u32[]{:S(2)}, u32[]{:S(2)}) collective-permute-start(f32[256,128]{1,0:T(8,128)S(1)} %fusion.refs_0_), channel_id=1, source_target_pairs={{0,1},{1,0},{2,3},{3,2},{4,5},{5,4},{6,7},{7,6},{8,9},{9,8},{10,11... | collective-permute-start | bytes 393224 | tf_op jit(solution)/shard_map/ppermute | solution.py:460
  155.1 9.5 %collective-permute-start.10 = (f32[256,128]{1,0:T(8,128)S(1)}, f32[256,128]{1,0:T(8,128)S(1)}, u32[]{:S(2)}, u32[]{:S(2)}) collective-permute-start(f32[256,128]{1,0:T(8,128)S(1)} %fusion.refs_0_), channel_id=1, source_target_pairs={{0,2},{1,3},{2,0},{3,1},{4,6},{5,7},{6,4},{7,5},{8,10},{9,11},{10,... | collective-permute-start | bytes 393224 | tf_op jit(solution)/shard_map/ppermute | solution.py:460
  156.8 8.7 %collective-permute-start.11 = (f32[256,128]{1,0:T(8,128)S(1)}, f32[256,128]{1,0:T(8,128)S(1)}, u32[]{:S(2)}, u32[]{:S(2)}) collective-permute-start(f32[256,128]{1,0:T(8,128)S(1)} %fusion.refs_0_), channel_id=1, source_target_pairs={{0,3},{1,2},{2,1},{3,0},{4,7},{5,6},{6,5},{7,4},{8,11},{9,10},{10,... | collective-permute-start | bytes 393224 | tf_op jit(solution)/shard_map/ppermute | solution.py:460
  161.1 7.7 %collective-permute-start.13 = (f32[256,128]{1,0:T(8,128)S(1)}, f32[256,128]{1,0:T(8,128)S(1)}, u32[]{:S(2)}, u32[]{:S(2)}) collective-permute-start(f32[256,128]{1,0:T(8,128)S(1)} %collective-permute-done.12.refs_0_), channel_id=1, source_target_pairs={{0,1},{1,0},{2,3},{3,2},{4,5},{5,4},{6,7},{7,6},{8,9},{9,8},{10,11... | collective-permute-start | bytes 393224 | tf_op jit(solution)/shard_map/ppermute | solution.py:460
  162.4 6.4 %collective-permute-start.14 = (f32[256,128]{1,0:T(8,128)S(1)}, f32[256,128]{1,0:T(8,128)S(1)}, u32[]{:S(2)}, u32[]{:S(2)}) collective-permute-start(f32[256,128]{1,0:T(8,128)S(1)} %collective-permute-done.12.refs_0_), channel_id=1, source_target_pairs={{0,2},{1,3},{2,0},{3,1},{4,6},{5,7},{6,4},{7,5},{8,10},{9,11},{10,... | collective-permute-start | bytes 393224 | tf_op jit(solution)/shard_map/ppermute | solution.py:460
  162.4 8.3 %collective-permute-start.15 = (f32[256,128]{1,0:T(8,128)S(1)}, f32[256,128]{1,0:T(8,128)S(1)}, u32[]{:S(2)}, u32[]{:S(2)}) collective-permute-start(f32[256,128]{1,0:T(8,128)S(1)} %collective-permute-done.12.refs_0_), channel_id=1, source_target_pairs={{0,3},{1,2},{2,1},{3,0},{4,7},{5,6},{6,5},{7,4},{8,11},{9,10},{10,... | collective-permute-start | bytes 393224 | tf_op jit(solution)/shard_map/ppermute | solution.py:460
  171.9 1.6 collective-permute-start.16
  173.6 5.6 %collective-permute-start.17 = (f32[1,256,128]{2,1,0:T(8,128)S(1)}, f32[1,256,128]{2,1,0:T(8,128)S(1)}, u32[]{:S(2)}, u32[]{:S(2)}) collective-permute-start(f32[1,256,128]{2,1,0:T(8,128)S(1)} %slice.32), channel_id=1, source_target_pairs={{0,16},{8,24},{16,0},{24,8},{1,17},{9,25},{17,1},{25,9},{2,18},{10... | collective-permute-start | bytes 393224 | tf_op jit(solution)/shard_map/ppermute | solution.py:460
